TPU v7x, 256 devices: a whole 4x4x8 slice. The times are simulated.
256 devices in a mesh: dp: 8 (over x, z_hi), expert: 32 (over z_lo, y, core).
Axes of the slice: x: 4, y: 4, z: 8 (z_hi: 2, z_lo: 4; z = z_hi * 4 + z_lo), core: 2. Of those that a mesh axis runs over, the one named last changes fastest.
Arguments:
- tokens: bfloat16 [32768, 5120], P(('dp', 'expert')), may hold values from -6 to 6
- cotangent: bfloat16 [32768, 5120], P(('dp', 'expert')), may hold values from -2 to 2
- picks: int32 [256, 32, 4], P(('dp', 'expert')), may hold values from 0 to 127, as said below
- gates: float32 [256, 32, 4], P(('dp', 'expert')), may hold values from 0.05 to 1
- w_gate: bfloat16 [32, 5120, 768], P('expert', 'dp'), may hold values from -0.078125 to 0.078125
- w_up: bfloat16 [32, 5120, 768], P('expert', 'dp'), may hold values from -0.078125 to 0.078125
- w_down: bfloat16 [32, 768, 5120], P('expert', None, 'dp'), may hold values from -0.21875 to 0.21875
Outputs:
- mixed: bfloat16 [32768, 5120], P(('dp', 'expert'))
- token_grad: bfloat16 [32768, 5120], P(('dp', 'expert'))
- gate_grad: float32 [256, 32, 4], P(('dp', 'expert'))
- grad_w_gate: bfloat16 [32, 5120, 768], P('expert', 'dp')
- grad_w_up: bfloat16 [32, 5120, 768], P('expert', 'dp')
- grad_w_down: bfloat16 [32, 768, 5120], P('expert', None, 'dp')
Inputs may be any that keep to these rules, and one draw needn't show every extreme that they name: picks[d, e] holds 4 distinct token indices of device d; every expert takes exactly 4 tokens from every device.
All inputs are finite; a program needn't handle non-finite values.
Results may differ from a plain program's by a relative error of at most 0.02.
Values may be sent and summed in bfloat16 or wider, within the bound.
A program may use at most 64 MiB of HBM per device.

v0:
```python
import jax
import jax.numpy as jnp
from jax import lax
from jax.sharding import PartitionSpec as P


def contract_rows(left, right):
    return lax.dot_general(
        left, right, (((0,), (0,)), ((), ())), preferred_element_type=jnp.float32
    )


def contract_cols(left, right):
    return lax.dot_general(
        left, right, (((1,), (1,)), ((), ())), preferred_element_type=jnp.float32
    )


def rounded(values):
    return lax.optimization_barrier(values.astype(jnp.bfloat16)).astype(jnp.float32)


def swiglu_grads(column_sums, hidden_units):
    gate_sum = column_sums[:, :hidden_units]
    up_sum = column_sums[:, hidden_units : 2 * hidden_units]
    back_sum = column_sums[:, 2 * hidden_units :]
    sigmoid_gate = jax.nn.sigmoid(gate_sum)
    silu_gate = gate_sum * sigmoid_gate
    hidden = (silu_gate * up_sum).astype(jnp.bfloat16)
    grad_up = (back_sum * silu_gate).astype(jnp.bfloat16)
    grad_gate = (back_sum * up_sum * sigmoid_gate * (1.0 + gate_sum * (1.0 - sigmoid_gate))).astype(
        jnp.bfloat16
    )
    return (hidden, grad_gate, grad_up)


def body(tokens, cotangent, picks, gates, w_gate, w_up, w_down):
    expert_count = picks.shape[1]
    slot_count = picks.shape[2]
    model_width = tokens.shape[1]
    chosen = picks[0].reshape(-1)
    scales = gates[0].reshape(-1)
    token_rows = jnp.take(tokens, chosen, axis=0)
    grad_rows = jnp.take(cotangent, chosen, axis=0)
    scaled_grad = (scales[:, None] * grad_rows.astype(jnp.float32)).astype(jnp.bfloat16)
    outgoing = (
        token_rows.reshape(expert_count, slot_count, model_width),
        scaled_grad.reshape(expert_count, slot_count, model_width),
    )
    arrived_in, arrived_up = (
        lax.all_to_all(
            lax.all_to_all(outgoing[0], "dp", split_axis=2, concat_axis=1, tiled=True),
            "expert",
            split_axis=0,
            concat_axis=0,
            tiled=True,
        ),
        lax.all_to_all(
            lax.all_to_all(outgoing[1], "dp", split_axis=2, concat_axis=1, tiled=True),
            "expert",
            split_axis=0,
            concat_axis=0,
            tiled=True,
        ),
    )
    arrived_shape = arrived_in.shape
    row_count = arrived_shape[0] * arrived_shape[1]
    slice_width = arrived_shape[2]
    inputs = arrived_in.reshape(row_count, slice_width)
    upstream = arrived_up.reshape(row_count, slice_width)
    gate_mat = w_gate[0]
    up_mat = w_up[0]
    down_mat = w_down[0]
    hidden_units = gate_mat.shape[1]
    terms = jnp.concatenate(
        [
            rounded(jnp.dot(inputs, gate_mat, preferred_element_type=jnp.float32)),
            rounded(jnp.dot(inputs, up_mat, preferred_element_type=jnp.float32)),
            rounded(contract_cols(upstream, down_mat)),
        ],
        axis=1,
    )
    shares = lax.psum_scatter(
        terms.astype(jnp.bfloat16), "dp", scatter_dimension=0, tiled=True
    ).astype(jnp.float32)
    own_hidden, own_grad_gate, own_grad_up = swiglu_grads(shares, hidden_units)
    hidden, grad_gate, grad_up = (
        lax.all_gather(own_hidden, "dp", axis=0, tiled=True),
        lax.all_gather(own_grad_gate, "dp", axis=0, tiled=True),
        lax.all_gather(own_grad_up, "dp", axis=0, tiled=True),
    )
    expert_out = jnp.dot(hidden, down_mat, preferred_element_type=jnp.float32).astype(jnp.bfloat16)
    input_grad = (contract_cols(grad_gate, gate_mat) + contract_cols(grad_up, up_mat)).astype(
        jnp.bfloat16
    )
    grad_down = contract_rows(hidden, upstream).astype(jnp.bfloat16)[None]
    grad_gate_w = contract_rows(inputs, grad_gate).astype(jnp.bfloat16)[None]
    grad_up_w = contract_rows(inputs, grad_up).astype(jnp.bfloat16)[None]
    back_out, back_grad = (
        lax.all_to_all(
            lax.all_to_all(
                expert_out.reshape(arrived_shape), "dp", split_axis=1, concat_axis=2, tiled=True
            ),
            "expert",
            split_axis=0,
            concat_axis=0,
            tiled=True,
        ),
        lax.all_to_all(
            lax.all_to_all(
                input_grad.reshape(arrived_shape), "dp", split_axis=1, concat_axis=2, tiled=True
            ),
            "expert",
            split_axis=0,
            concat_axis=0,
            tiled=True,
        ),
    )
    back_out = back_out.reshape(expert_count * slot_count, model_width)
    back_grad = back_grad.reshape(expert_count * slot_count, model_width)
    positions = jnp.arange(tokens.shape[0], dtype=jnp.int32)
    select = chosen[:, None] == positions[None, :]
    weighted = jnp.where(select, scales[:, None], jnp.float32(0.0))
    out_float = back_out.astype(jnp.float32)
    mixed = lax.dot_general(
        weighted,
        out_float,
        (((0,), (0,)), ((), ())),
        precision=lax.Precision.HIGHEST,
        preferred_element_type=jnp.float32,
    ).astype(jnp.bfloat16)
    token_grad = contract_rows(select.astype(jnp.bfloat16), back_grad).astype(jnp.bfloat16)
    gate_grad = jnp.sum(grad_rows.astype(jnp.float32) * out_float, axis=1).reshape(
        1, expert_count, slot_count
    )
    return (mixed, token_grad, gate_grad, grad_gate_w, grad_up_w, grad_down)


def solution(mesh):
    return jax.shard_map(
        body,
        mesh=mesh,
        in_specs=(
            P(("dp", "expert"), None),
            P(("dp", "expert"), None),
            P(("dp", "expert"), None, None),
            P(("dp", "expert"), None, None),
            P("expert", "dp", None),
            P("expert", "dp", None),
            P("expert", None, "dp"),
        ),
        out_specs=(
            P(("dp", "expert"), None),
            P(("dp", "expert"), None),
            P(("dp", "expert"), None, None),
            P("expert", "dp", None),
            P("expert", "dp", None),
            P("expert", None, "dp"),
        ),
        check_vma=False,
    )
```

profile of v0, /device:TPU:1, one launch (start us, length us, event | category | flops | bytes accessed | tf_op | source)
XLA Modules:
  0.0 669.9 jit_solution(6501620156101534513)
XLA Ops:
  12.1 8.8 %copy.79 = bf16[32,4,5120]{0,1,2:T(4,128)(2,1)} copy(bf16[32,4,5120]{2,1,0:T(4,128)(2,1)} %reshape.48) | data formatting | bytes 2621440 | tf_op jit(solution)/shard_map/reshape | solution.py:48
  20.9 8.6 %reshape.77 = bf16[8,2,40960]{2,1,0:T(2,128)(2,1)} reshape(bf16[5120,4,32]{2,1,0:T(4,128)(2,1)} %bitcast.66) | data formatting | bytes 2621440
  29.5 11.6 %all-to-all-start.2 = ((bf16[8,2,40960]{2,1,0:T(2,128)(2,1)}), bf16[8,2,40960]{2,1,0:T(2,128)(2,1)}, u32[]{:S(2)}, u32[]{:S(2)}) async-start(bf16[8,2,40960]{2,1,0:T(2,128)(2,1)} %reshape.77), calls=%async_computation.2 | async-start | bytes 2621440 | tf_op jit(solution)/shard_map/all_to_all | solution.py:59
  41.1 2.4 gather_fusion
  43.5 1.5 broadcast_select_fusion.1
  46.3 8.8 %copy.75 = bf16[32,4,5120]{0,1,2:T(4,128)(2,1)} copy(bf16[32,4,5120]{2,1,0:T(4,128)(2,1)} %reshape.46) | data formatting | bytes 2621440 | tf_op jit(solution)/shard_map/reshape | solution.py:47
  55.1 8.7 %reshape.79 = bf16[8,2,40960]{2,1,0:T(2,128)(2,1)} reshape(bf16[5120,4,32]{2,1,0:T(4,128)(2,1)} %bitcast.67) | data formatting | bytes 2621440
  63.7 2.6 all-to-all-done.2
  66.4 6.4 all-to-all-start
  72.8 7.5 %reshape.78 = bf16[5120,4,32]{2,1,0:T(4,128)(2,1)} reshape(bf16[8,2,40960]{2,1,0:T(2,128)(2,1)} %all-to-all-done.2) | data formatting | bytes 2621440
  80.3 7.1 %copy.92 = bf16[32,4,8,640]{3,0,1,2:T(8,128)(2,1)} copy(bf16[32,4,8,640]{0,1,3,2:T(4,128)(2,1)} %bitcast.68) | data formatting | bytes 2621440 | tf_op jit(solution)/shard_map/all_to_all | solution.py:59
  87.5 2.8 copy.82
  90.2 3.4 all-to-all-done
  93.6 23.1 %all-to-all-start.3 = ((bf16[32,32,640]{2,1,0:T(8,128)(2,1)}), bf16[32,32,640]{2,1,0:T(8,128)(2,1)}, u32[]{:S(2)}, u32[]{:S(2)}) async-start(bf16[32,32,640]{2,1,0:T(8,128)(2,1)} %copy.82), calls=%async_computation.3 | async-start | bytes 2621440 | tf_op jit(solution)/shard_map/all_to_all | solution.py:58
  116.7 5.0 reshape.80
  121.7 6.0 copy.90
  129.2 19.3 %all-to-all-done.3 = bf16[32,32,640]{2,1,0:T(8,128)(2,1)} async-done(((bf16[32,32,640]{2,1,0:T(8,128)(2,1)}), bf16[32,32,640]{2,1,0:T(8,128)(2,1)}, u32[]{:S(2)}, u32[]{:S(2)}) %all-to-all-start.3) | async-done | bytes 1310752 | tf_op jit(solution)/shard_map/all_to_all | solution.py:58
  148.5 5.6 all-to-all-start.1
  154.2 4.2 convolution_convert_fusion.2
  158.4 27.5 %all-to-all-done.1 = bf16[32,32,640]{2,1,0:T(8,128)(2,1)S(1)} async-done(((bf16[32,32,640]{2,1,0:T(8,128)(2,1)}), bf16[32,32,640]{2,1,0:T(8,128)(2,1)S(1)}, u32[]{:S(2)}, u32[]{:S(2)}) %all-to-all-start.1) | async-done | bytes 1310752 | tf_op jit(solution)/shard_map/all_to_all | solution.py:51
  185.9 3.1 convolution_convert_fusion.3
  190.4 2.3 pad_maximum_fusion
  192.8 125.3 %reduce-scatter.2.cloned.1.call-done = bf16[128,2304]{1,0:T(8,128)(2,1)} async-done(((bf16[1024,2304]{1,0:T(8,128)(2,1)}), bf16[128,2304]{1,0:T(8,128)(2,1)}) %reduce-scatter.2.cloned.1.call-update) | async-done | bytes 589840 | tf_op jit(solution)/shard_map/reduce_scatter | solution.py:83
  321.6 62.8 %all-gather.4.cloned.1.call-done = bf16[1024,768]{1,0:T(8,128)(2,1)} async-done(((bf16[128,768]{1,0:T(8,128)(2,1)}), bf16[1024,768]{1,0:T(8,128)(2,1)}) %all-gather.4.cloned.1.call-update) | async-done | bytes 1572880 | tf_op jit(solution)/shard_map/all_gather | solution.py:88
  384.4 3.1 convolution_convert_fusion.5
  389.0 3.7 all-to-all-start.4
  392.6 74.9 %all-gather.6.cloned.1.call-done = bf16[1024,768]{1,0:T(8,128)(2,1)} async-done(((bf16[128,768]{1,0:T(8,128)(2,1)}), bf16[1024,768]{1,0:T(8,128)(2,1)}) %all-gather.6.cloned.1.call-update) | async-done | bytes 1572880 | tf_op jit(solution)/shard_map/all_gather | solution.py:89
  467.5 4.6 fusion.9
  472.1 63.2 %all-gather.8.cloned.1.call-done = bf16[1024,768]{1,0:T(8,128)(2,1)} async-done(((bf16[128,768]{1,0:T(8,128)(2,1)}), bf16[1024,768]{1,0:T(8,128)(2,1)}) %all-gather.8.cloned.1.call-update) | async-done | bytes 1572880 | tf_op jit(solution)/shard_map/all_gather | solution.py:90
  535.3 3.9 add_convert_fusion
  540.8 4.3 all-to-all-start.6
  545.0 1.8 copy.84
  546.8 3.6 all_to_all.77
  550.4 13.2 %all-to-all-done.6 = bf16[32,32,640]{2,0,1:T(8,128)(2,1)} async-done(((bf16[32,32,640]{2,0,1:T(8,128)(2,1)}), bf16[32,32,640]{2,0,1:T(8,128)(2,1)}, u32[]{:S(2)}, u32[]{:S(2)}) %all-to-all-start.6) | async-done | bytes 1310752 | tf_op jit(solution)/shard_map/all_to_all | solution.py:110
  563.6 25.2 %all-to-all-start.5 = ((bf16[32,4,5120]{2,1,0:T(4,128)(2,1)}), bf16[32,4,5120]{2,1,0:T(4,128)(2,1)S(1)}, u32[]{:S(2)}, u32[]{:S(2)}) async-start(bf16[32,4,5120]{2,1,0:T(4,128)(2,1)} %all_to_all.77), calls=%async_computation.6 | async-start | bytes 2621440 | tf_op jit(solution)/shard_map/all_to_all | solution.py:100
  588.8 3.1 copy.94
  591.9 3.2 all_to_all.82
  595.1 3.4 copy.87
  598.5 22.0 %all-to-all-done.5 = bf16[32,4,5120]{2,1,0:T(4,128)(2,1)S(1)} async-done(((bf16[32,4,5120]{2,1,0:T(4,128)(2,1)}), bf16[32,4,5120]{2,1,0:T(4,128)(2,1)S(1)}, u32[]{:S(2)}, u32[]{:S(2)}) %all-to-all-start.5) | async-done | bytes 1310752 | tf_op jit(solution)/shard_map/all_to_all | solution.py:100
  621.6 5.7 all-to-all-start.7
  627.3 4.3 fusion.4
  631.6 2.2 fusion.2
  633.9 2.2 fusion.3
  636.1 2.5 reshape.51
  639.9 2.4 convolution_convert_fusion.1
  642.2 16.8 %all-to-all-done.7 = bf16[32,4,5120]{2,1,0:T(4,128)(2,1)} async-done(((bf16[32,4,5120]{2,1,0:T(4,128)(2,1)}), bf16[32,4,5120]{2,1,0:T(4,128)(2,1)}, u32[]{:S(2)}, u32[]{:S(2)}) %all-to-all-start.7) | async-done | bytes 1310752 | tf_op jit(solution)/shard_map/all_to_all | solution.py:109
  659.1 2.6 reshape.53
  661.7 1.7 convolution_convert_fusion
  (49 shorter events, 18.1 us)
Async XLA Ops:
  7.2 1.9 copy-start
  29.5 11.6 %copy-start.2 = (bf16[128,5120]{1,0:T(8,128)(2,1)S(1)}, bf16[128,5120]{1,0:T(8,128)(2,1)}, u32[]{:S(2)}) copy-start(bf16[128,5120]{1,0:T(8,128)(2,1)} %param.9) | copy-start | bytes 3932164
  29.5 36.8 %all-to-all-start.2 = ((bf16[8,2,40960]{2,1,0:T(2,128)(2,1)}), bf16[8,2,40960]{2,1,0:T(2,128)(2,1)}, u32[]{:S(2)}, u32[]{:S(2)}) async-start(bf16[8,2,40960]{2,1,0:T(2,128)(2,1)} %reshape.77), calls=%async_computation.2 | async-start | bytes 2621440 | tf_op jit(solution)/shard_map/all_to_all | solution.py:59
  66.4 27.2 %all-to-all-start = ((bf16[8,2,40960]{2,1,0:T(2,128)(2,1)}), bf16[8,2,40960]{2,1,0:T(2,128)(2,1)S(1)}, u32[]{:S(2)}, u32[]{:S(2)}) async-start(bf16[8,2,40960]{2,1,0:T(2,128)(2,1)} %reshape.79), calls=%async_computation | async-start | bytes 2621440 | tf_op jit(solution)/shard_map/all_to_all | solution.py:52
  93.6 54.9 %all-to-all-start.3 = ((bf16[32,32,640]{2,1,0:T(8,128)(2,1)}), bf16[32,32,640]{2,1,0:T(8,128)(2,1)}, u32[]{:S(2)}, u32[]{:S(2)}) async-start(bf16[32,32,640]{2,1,0:T(8,128)(2,1)} %copy.82), calls=%async_computation.3 | async-start | bytes 2621440 | tf_op jit(solution)/shard_map/all_to_all | solution.py:58
  148.5 37.4 %all-to-all-start.1 = ((bf16[32,32,640]{2,1,0:T(8,128)(2,1)}), bf16[32,32,640]{2,1,0:T(8,128)(2,1)S(1)}, u32[]{:S(2)}, u32[]{:S(2)}) async-start(bf16[32,32,640]{2,1,0:T(8,128)(2,1)} %copy.78), calls=%async_computation.1 | async-start | bytes 2621440 | tf_op jit(solution)/shard_map/all_to_all | solution.py:51
  154.1 164.0 %reduce-scatter.2.cloned.1.call-start = ((), (), s32[]{:S(2)}) async-start(), calls=%async_computation.9 | async-start | bytes 5308416 | tf_op jit(solution)/shard_map/reduce_scatter | solution.py:83
  185.9 3.1 copy-start.5
  185.9 3.1 copy-start.9
  189.0 1.4 copy-start.4
  192.8 191.6 %all-gather.4.cloned.1.call-start = ((), (), s32[]{:S(2)}) async-start(), calls=%async_computation.10 | async-start | bytes 1769472 | tf_op jit(solution)/shard_map/all_gather | solution.py:88
  320.3 147.2 %all-gather.6.cloned.1.call-start = ((), (), s32[]{:S(2)}) async-start(), calls=%async_computation.11 | async-start | bytes 1769472 | tf_op jit(solution)/shard_map/all_gather | solution.py:89
  321.0 214.3 %all-gather.8.cloned.1.call-start = ((), (), s32[]{:S(2)}) async-start(), calls=%async_computation.12 | async-start | bytes 1769472 | tf_op jit(solution)/shard_map/all_gather | solution.py:90
  389.0 151.8 %all-to-all-start.4 = ((bf16[32,32,640]{2,0,1:T(8,128)(2,1)}), bf16[32,32,640]{2,0,1:T(8,128)(2,1)S(1)}, u32[]{:S(2)}, u32[]{:S(2)}) async-start(bf16[32,32,640]{2,0,1:T(8,128)(2,1)} %copy.83), calls=%async_computation.5 | async-start | bytes 2621440 | tf_op jit(solution)/shard_map/all_to_all | solution.py:101
  540.8 22.8 %all-to-all-start.6 = ((bf16[32,32,640]{2,0,1:T(8,128)(2,1)}), bf16[32,32,640]{2,0,1:T(8,128)(2,1)}, u32[]{:S(2)}, u32[]{:S(2)}) async-start(bf16[32,32,640]{2,0,1:T(8,128)(2,1)} %copy.85), calls=%async_computation.7 | async-start | bytes 2621440 | tf_op jit(solution)/shard_map/all_to_all | solution.py:110
  563.6 56.9 %all-to-all-start.5 = ((bf16[32,4,5120]{2,1,0:T(4,128)(2,1)}), bf16[32,4,5120]{2,1,0:T(4,128)(2,1)S(1)}, u32[]{:S(2)}, u32[]{:S(2)}) async-start(bf16[32,4,5120]{2,1,0:T(4,128)(2,1)} %all_to_all.77), calls=%async_computation.6 | async-start | bytes 2621440 | tf_op jit(solution)/shard_map/all_to_all | solution.py:100
  620.5 1.1 copy-start.3
  621.6 37.5 %all-to-all-start.7 = ((bf16[32,4,5120]{2,1,0:T(4,128)(2,1)}), bf16[32,4,5120]{2,1,0:T(4,128)(2,1)}, u32[]{:S(2)}, u32[]{:S(2)}) async-start(bf16[32,4,5120]{2,1,0:T(4,128)(2,1)} %copy.87), calls=%async_computation.8 | async-start | bytes 2621440 | tf_op jit(solution)/shard_map/all_to_all | solution.py:109
  627.3 4.3 copy-start.6
  627.3 4.3 copy-start.7
  631.6 2.2 copy-start.8
  659.1 4.2 copy-start.1
Sparse Core Ops, SparseCore 0:
  192.9 125.1 reduce-scatter.1
  321.3 63.1 all-gather.3
  387.6 79.8 all-gather.5
  470.5 64.7 all-gather.7
where the time goes:
time: 672 us; the launch traced here: 670 us
  waiting for transfers between devices  432 us (64%)
  local copies, waits for them, and re-layouts  97.9 us (15%)
  starting transfers between devices  85.9 us (13%)
  matrix products  33 us (5%)
  between operations  14 us (2%)
  other arithmetic  6.97 us (1%)
    reduce_scatter x1, waiting for transfers between devices, body(): lax.psum_scatter(terms.astype(jnp.bfloat16), 'dp', scatter_dimension=0, t...  125 us
    all_gather x1, waiting for transfers between devices, body(): lax.all_gather(own_grad_gate, 'dp', axis=0, tiled=True)  74.9 us
    all_gather x1, waiting for transfers between devices, body(): lax.all_gather(own_grad_up, 'dp', axis=0, tiled=True)  63.2 us
    all_gather x1, waiting for transfers between devices, body(): lax.all_gather(own_hidden, 'dp', axis=0, tiled=True)  62.8 us
    unnamed x27, local copies, waits for them, and re-layouts  33.2 us
    all_to_all x1, waiting for transfers between devices, body(): lax.all_to_all(lax.all_to_all(outgoing[0], 'dp', split_axis=2, concat_axi...  27.5 us
    all_to_all x1, starting transfers between devices, body(): lax.all_to_all(lax.all_to_all(expert_out.reshape(arrived_shape), 'dp', sp...  25.2 us
    all_to_all x1, starting transfers between devices, body(): lax.all_to_all(lax.all_to_all(outgoing[1], 'dp', split_axis=2, concat_axi...  23.1 us
  transfers between devices with their start and end apart: 12, of which 11 were waited for; matrix products, arithmetic and copies ran while one was open for 14% of the time, Pallas kernels for 0%

commit v1 on v0

--- a/solution.py
+++ b/solution.py
@@ -85,7 +85,9 @@
     ).astype(jnp.float32)
     own_hidden, own_grad_gate, own_grad_up = swiglu_grads(shares, hidden_units)
     hidden, grad_gate, grad_up = (
-        lax.all_gather(own_hidden, "dp", axis=0, tiled=True),
+        jnp.concatenate(
+            lax.all_to_all(jnp.stack([own_hidden] * lax.axis_size("dp")), "dp", 0, 0), axis=0
+        ),
         lax.all_gather(own_grad_gate, "dp", axis=0, tiled=True),
         lax.all_gather(own_grad_up, "dp", axis=0, tiled=True),
     )

time: 672 us -> 623 us (0.927)
  waiting for transfers between devices: 432 us -> 377 us
    all_gather x1 -> x0, waiting for transfers between devices: 62.8 us -> none  [body(): lax.all_gather(own_hidden, 'dp', axis=0, tiled=True)]
    all_gather x1, waiting for transfers between devices: 74.9 us -> 37 us  [body(): lax.all_gather(own_grad_gate, 'dp', axis=0, tiled=True)]
    all_to_all x0 -> x1, waiting for transfers between devices: none -> 27.3 us  [body(): lax.all_to_all(jnp.stack([own_hidden] * lax.axis_size('dp')), 'dp', 0, 0)]
    all_gather x1, waiting for transfers between devices: 63.2 us -> 83.1 us  [body(): lax.all_gather(own_grad_up, 'dp', axis=0, tiled=True)]
  transfers between devices with their start and end apart: 12 -> 12, of which waited for: 11 -> 11; matrix products, arithmetic and copies ran while one was open for 14% -> 15% of each run, Pallas kernels for 0% -> 0%
where the time goes in v1:
time: 623 us; the launch traced here: 620 us
  waiting for transfers between devices  377 us (61%)
  local copies, waits for them, and re-layouts  99.2 us (16%)
  starting transfers between devices  90.1 us (14%)
  matrix products  33.1 us (5%)
  between operations  14 us (2%)
  other arithmetic  6.93 us (1%)
    reduce_scatter x1, waiting for transfers between devices, body(): lax.psum_scatter(terms.astype(jnp.bfloat16), 'dp', scatter_dimension=0, t...  123 us
    all_gather x1, waiting for transfers between devices, body(): lax.all_gather(own_grad_up, 'dp', axis=0, tiled=True)  83.1 us
    all_gather x1, waiting for transfers between devices, body(): lax.all_gather(own_grad_gate, 'dp', axis=0, tiled=True)  37 us
    unnamed x27, local copies, waits for them, and re-layouts  33.3 us
    all_to_all x1, waiting for transfers between devices, body(): lax.all_to_all(lax.all_to_all(outgoing[0], 'dp', split_axis=2, concat_axi...  27.5 us
    all_to_all x1, waiting for transfers between devices, body(): lax.all_to_all(jnp.stack([own_hidden] * lax.axis_size('dp')), 'dp', 0, 0)  27.3 us
    all_to_all x1, starting transfers between devices, body(): lax.all_to_all(lax.all_to_all(expert_out.reshape(arrived_shape), 'dp', sp...  25.2 us
    all_to_all x1, starting transfers between devices, body(): lax.all_to_all(lax.all_to_all(outgoing[1], 'dp', split_axis=2, concat_axi...  23.1 us
  transfers between devices with their start and end apart: 12, of which 11 were waited for; matrix products, arithmetic and copies ran while one was open for 15% of the time, Pallas kernels for 0%

profile of v1, /device:TPU:1, one launch (start us, length us, event | category | flops | bytes accessed | tf_op | source)
XLA Modules:
  0.0 620.5 jit_solution(17290799600068056550)
XLA Ops:
  12.1 8.7 %copy.79 = bf16[32,4,5120]{0,1,2:T(4,128)(2,1)} copy(bf16[32,4,5120]{2,1,0:T(4,128)(2,1)} %reshape.53) | data formatting | bytes 2621440 | tf_op jit(solution)/shard_map/reshape | solution.py:48
  20.9 8.6 %reshape.83 = bf16[8,2,40960]{2,1,0:T(2,128)(2,1)} reshape(bf16[5120,4,32]{2,1,0:T(4,128)(2,1)} %bitcast.67) | data formatting | bytes 2621440
  29.5 11.6 %all-to-all-start.2 = ((bf16[8,2,40960]{2,1,0:T(2,128)(2,1)}), bf16[8,2,40960]{2,1,0:T(2,128)(2,1)}, u32[]{:S(2)}, u32[]{:S(2)}) async-start(bf16[8,2,40960]{2,1,0:T(2,128)(2,1)} %reshape.83), calls=%async_computation.2 | async-start | bytes 2621440 | tf_op jit(solution)/shard_map/all_to_all | solution.py:59
  41.1 2.4 gather_fusion
  46.3 8.7 %copy.75 = bf16[32,4,5120]{0,1,2:T(4,128)(2,1)} copy(bf16[32,4,5120]{2,1,0:T(4,128)(2,1)} %reshape.51) | data formatting | bytes 2621440 | tf_op jit(solution)/shard_map/reshape | solution.py:47
  55.1 8.7 %reshape.85 = bf16[8,2,40960]{2,1,0:T(2,128)(2,1)} reshape(bf16[5120,4,32]{2,1,0:T(4,128)(2,1)} %bitcast.68) | data formatting | bytes 2621440
  63.7 2.6 all-to-all-done.2
  66.3 6.4 %all-to-all-start = ((bf16[8,2,40960]{2,1,0:T(2,128)(2,1)}), bf16[8,2,40960]{2,1,0:T(2,128)(2,1)S(1)}, u32[]{:S(2)}, u32[]{:S(2)}) async-start(bf16[8,2,40960]{2,1,0:T(2,128)(2,1)} %reshape.85), calls=%async_computation | async-start | bytes 2621440 | tf_op jit(solution)/shard_map/all_to_all | solution.py:52
  72.8 7.5 %reshape.84 = bf16[5120,4,32]{2,1,0:T(4,128)(2,1)} reshape(bf16[8,2,40960]{2,1,0:T(2,128)(2,1)} %all-to-all-done.2) | data formatting | bytes 2621440
  80.3 7.1 %copy.92 = bf16[32,4,8,640]{3,0,1,2:T(8,128)(2,1)} copy(bf16[32,4,8,640]{0,1,3,2:T(4,128)(2,1)} %bitcast.69) | data formatting | bytes 2621440 | tf_op jit(solution)/shard_map/all_to_all | solution.py:59
  87.4 2.8 copy.82
  90.2 3.4 all-to-all-done
  93.6 23.1 %all-to-all-start.3 = ((bf16[32,32,640]{2,1,0:T(8,128)(2,1)}), bf16[32,32,640]{2,1,0:T(8,128)(2,1)}, u32[]{:S(2)}, u32[]{:S(2)}) async-start(bf16[32,32,640]{2,1,0:T(8,128)(2,1)} %copy.82), calls=%async_computation.3 | async-start | bytes 2621440 | tf_op jit(solution)/shard_map/all_to_all | solution.py:58
  116.7 5.0 reshape.86
  121.7 6.0 copy.90
  129.2 19.2 %all-to-all-done.3 = bf16[32,32,640]{2,1,0:T(8,128)(2,1)} async-done(((bf16[32,32,640]{2,1,0:T(8,128)(2,1)}), bf16[32,32,640]{2,1,0:T(8,128)(2,1)}, u32[]{:S(2)}, u32[]{:S(2)}) %all-to-all-start.3) | async-done | bytes 1310752 | tf_op jit(solution)/shard_map/all_to_all | solution.py:58
  148.5 5.6 all-to-all-start.1
  154.2 4.2 convolution_convert_fusion.2
  158.4 27.5 %all-to-all-done.1 = bf16[32,32,640]{2,1,0:T(8,128)(2,1)S(1)} async-done(((bf16[32,32,640]{2,1,0:T(8,128)(2,1)}), bf16[32,32,640]{2,1,0:T(8,128)(2,1)S(1)}, u32[]{:S(2)}, u32[]{:S(2)}) %all-to-all-start.1) | async-done | bytes 1310752 | tf_op jit(solution)/shard_map/all_to_all | solution.py:51
  185.9 3.1 convolution_convert_fusion.3
  190.4 2.3 pad_maximum_fusion
  192.8 123.5 %reduce-scatter.2.cloned.1.call-done = bf16[128,2304]{1,0:T(8,128)(2,1)} async-done(((bf16[1024,2304]{1,0:T(8,128)(2,1)}), bf16[128,2304]{1,0:T(8,128)(2,1)}) %reduce-scatter.2.cloned.1.call-update) | async-done | bytes 589840 | tf_op jit(solution)/shard_map/reduce_scatter | solution.py:83
  319.8 4.5 all-to-all-start.4
  325.0 27.3 %all-to-all-done.4 = bf16[8,128,768]{2,1,0:T(8,128)(2,1)} async-done(((bf16[8,128,768]{2,1,0:T(8,128)(2,1)}), bf16[8,128,768]{2,1,0:T(8,128)(2,1)}, u32[]{:S(2)}, u32[]{:S(2)}) %all-to-all-start.4) | async-done | bytes 1572896 | tf_op jit(solution)/shard_map/all_to_all | solution.py:89
  352.3 3.1 convolution_convert_fusion.5
  356.9 3.6 all-to-all-start.5
  360.4 37.0 %all-gather.3.cloned.1.call-done = bf16[1024,768]{1,0:T(8,128)(2,1)} async-done(((bf16[128,768]{1,0:T(8,128)(2,1)}), bf16[1024,768]{1,0:T(8,128)(2,1)}) %all-gather.3.cloned.1.call-update) | async-done | bytes 1572880 | tf_op jit(solution)/shard_map/all_gather | solution.py:91
  397.4 4.6 fusion.9
  402.0 83.1 %all-gather.5.cloned.1.call-done = bf16[1024,768]{1,0:T(8,128)(2,1)} async-done(((bf16[128,768]{1,0:T(8,128)(2,1)}), bf16[1024,768]{1,0:T(8,128)(2,1)}) %all-gather.5.cloned.1.call-update) | async-done | bytes 1572880 | tf_op jit(solution)/shard_map/all_gather | solution.py:92
  485.2 3.9 add_convert_fusion
  490.6 4.3 all-to-all-start.7
  494.9 1.8 copy.84
  496.7 3.6 all_to_all.81
  500.3 13.2 %all-to-all-done.7 = bf16[32,32,640]{2,0,1:T(8,128)(2,1)} async-done(((bf16[32,32,640]{2,0,1:T(8,128)(2,1)}), bf16[32,32,640]{2,0,1:T(8,128)(2,1)}, u32[]{:S(2)}, u32[]{:S(2)}) %all-to-all-start.7) | async-done | bytes 1310752 | tf_op jit(solution)/shard_map/all_to_all | solution.py:112
  513.4 25.2 %all-to-all-start.6 = ((bf16[32,4,5120]{2,1,0:T(4,128)(2,1)}), bf16[32,4,5120]{2,1,0:T(4,128)(2,1)S(1)}, u32[]{:S(2)}, u32[]{:S(2)}) async-start(bf16[32,4,5120]{2,1,0:T(4,128)(2,1)} %all_to_all.81), calls=%async_computation.7 | async-start | bytes 2621440 | tf_op jit(solution)/shard_map/all_to_all | solution.py:102
  538.6 3.1 copy.94
  541.7 3.2 all_to_all.86
  545.0 3.4 copy.87
  548.4 22.0 %all-to-all-done.6 = bf16[32,4,5120]{2,1,0:T(4,128)(2,1)S(1)} async-done(((bf16[32,4,5120]{2,1,0:T(4,128)(2,1)}), bf16[32,4,5120]{2,1,0:T(4,128)(2,1)S(1)}, u32[]{:S(2)}, u32[]{:S(2)}) %all-to-all-start.6) | async-done | bytes 1310752 | tf_op jit(solution)/shard_map/all_to_all | solution.py:102
  571.4 5.7 all-to-all-start.8
  577.2 4.3 fusion.4
  581.5 2.2 fusion.2
  583.7 2.2 fusion.3
  585.9 2.5 reshape.57
  589.0 2.4 convolution_convert_fusion.1
  591.3 17.6 %all-to-all-done.8 = bf16[32,4,5120]{2,1,0:T(4,128)(2,1)} async-done(((bf16[32,4,5120]{2,1,0:T(4,128)(2,1)}), bf16[32,4,5120]{2,1,0:T(4,128)(2,1)}, u32[]{:S(2)}, u32[]{:S(2)}) %all-to-all-start.8) | async-done | bytes 1310752 | tf_op jit(solution)/shard_map/all_to_all | solution.py:111
  608.9 2.6 reshape.59
  611.5 1.7 convolution_convert_fusion
  (49 shorter events, 20.2 us)
Async XLA Ops:
  7.2 1.9 copy-start
  29.5 11.6 %copy-start.2 = (bf16[128,5120]{1,0:T(8,128)(2,1)S(1)}, bf16[128,5120]{1,0:T(8,128)(2,1)}, u32[]{:S(2)}) copy-start(bf16[128,5120]{1,0:T(8,128)(2,1)} %param.9) | copy-start | bytes 3932164
  29.5 36.8 %all-to-all-start.2 = ((bf16[8,2,40960]{2,1,0:T(2,128)(2,1)}), bf16[8,2,40960]{2,1,0:T(2,128)(2,1)}, u32[]{:S(2)}, u32[]{:S(2)}) async-start(bf16[8,2,40960]{2,1,0:T(2,128)(2,1)} %reshape.83), calls=%async_computation.2 | async-start | bytes 2621440 | tf_op jit(solution)/shard_map/all_to_all | solution.py:59
  66.3 27.2 %all-to-all-start = ((bf16[8,2,40960]{2,1,0:T(2,128)(2,1)}), bf16[8,2,40960]{2,1,0:T(2,128)(2,1)S(1)}, u32[]{:S(2)}, u32[]{:S(2)}) async-start(bf16[8,2,40960]{2,1,0:T(2,128)(2,1)} %reshape.85), calls=%async_computation | async-start | bytes 2621440 | tf_op jit(solution)/shard_map/all_to_all | solution.py:52
  93.6 54.9 %all-to-all-start.3 = ((bf16[32,32,640]{2,1,0:T(8,128)(2,1)}), bf16[32,32,640]{2,1,0:T(8,128)(2,1)}, u32[]{:S(2)}, u32[]{:S(2)}) async-start(bf16[32,32,640]{2,1,0:T(8,128)(2,1)} %copy.82), calls=%async_computation.3 | async-start | bytes 2621440 | tf_op jit(solution)/shard_map/all_to_all | solution.py:58
  148.5 37.4 %all-to-all-start.1 = ((bf16[32,32,640]{2,1,0:T(8,128)(2,1)}), bf16[32,32,640]{2,1,0:T(8,128)(2,1)S(1)}, u32[]{:S(2)}, u32[]{:S(2)}) async-start(bf16[32,32,640]{2,1,0:T(8,128)(2,1)} %copy.78), calls=%async_computation.1 | async-start | bytes 2621440 | tf_op jit(solution)/shard_map/all_to_all | solution.py:51
  154.1 162.2 %reduce-scatter.2.cloned.1.call-start = ((), (), s32[]{:S(2)}) async-start(), calls=%async_computation.10 | async-start | bytes 5308416 | tf_op jit(solution)/shard_map/reduce_scatter | solution.py:83
  185.9 3.1 copy-start.5
  185.9 3.1 copy-start.9
  189.0 1.4 copy-start.4
  192.8 204.7 %all-gather.3.cloned.1.call-start = ((), (), s32[]{:S(2)}) async-start(), calls=%async_computation.11 | async-start | bytes 1769472 | tf_op jit(solution)/shard_map/all_gather | solution.py:91
  319.8 32.6 %all-to-all-start.4 = ((bf16[8,128,768]{2,1,0:T(8,128)(2,1)}), bf16[8,128,768]{2,1,0:T(8,128)(2,1)}, u32[]{:S(2)}, u32[]{:S(2)}) async-start(bf16[8,128,768]{2,1,0:T(8,128)(2,1)} %stack.2), calls=%async_computation.5 | async-start | bytes 3145728 | tf_op jit(solution)/shard_map/all_to_all | solution.py:89
  324.2 160.9 %all-gather.5.cloned.1.call-start = ((), (), s32[]{:S(2)}) async-start(), calls=%async_computation.12 | async-start | bytes 1769472 | tf_op jit(solution)/shard_map/all_gather | solution.py:92
  356.9 133.8 %all-to-all-start.5 = ((bf16[32,32,640]{2,0,1:T(8,128)(2,1)}), bf16[32,32,640]{2,0,1:T(8,128)(2,1)S(1)}, u32[]{:S(2)}, u32[]{:S(2)}) async-start(bf16[32,32,640]{2,0,1:T(8,128)(2,1)} %copy.83), calls=%async_computation.6 | async-start | bytes 2621440 | tf_op jit(solution)/shard_map/all_to_all | solution.py:103
  490.6 22.8 %all-to-all-start.7 = ((bf16[32,32,640]{2,0,1:T(8,128)(2,1)}), bf16[32,32,640]{2,0,1:T(8,128)(2,1)}, u32[]{:S(2)}, u32[]{:S(2)}) async-start(bf16[32,32,640]{2,0,1:T(8,128)(2,1)} %copy.85), calls=%async_computation.8 | async-start | bytes 2621440 | tf_op jit(solution)/shard_map/all_to_all | solution.py:112
  513.4 56.9 %all-to-all-start.6 = ((bf16[32,4,5120]{2,1,0:T(4,128)(2,1)}), bf16[32,4,5120]{2,1,0:T(4,128)(2,1)S(1)}, u32[]{:S(2)}, u32[]{:S(2)}) async-start(bf16[32,4,5120]{2,1,0:T(4,128)(2,1)} %all_to_all.81), calls=%async_computation.7 | async-start | bytes 2621440 | tf_op jit(solution)/shard_map/all_to_all | solution.py:102
  570.4 1.1 copy-start.3
  571.4 37.5 %all-to-all-start.8 = ((bf16[32,4,5120]{2,1,0:T(4,128)(2,1)}), bf16[32,4,5120]{2,1,0:T(4,128)(2,1)}, u32[]{:S(2)}, u32[]{:S(2)}) async-start(bf16[32,4,5120]{2,1,0:T(4,128)(2,1)} %copy.87), calls=%async_computation.9 | async-start | bytes 2621440 | tf_op jit(solution)/shard_map/all_to_all | solution.py:111
  577.1 4.3 copy-start.6
  577.1 4.3 copy-start.7
  581.5 2.2 copy-start.8
  608.9 5.0 copy-start.1
Sparse Core Ops, SparseCore 0:
  192.9 123.3 reduce-scatter.1
  319.5 77.8 all-gather.2
  400.6 84.5 all-gather.4
